TPU v7x, 32 devices: a whole 2x2x4 slice. The times are simulated.
32 devices in a mesh: dom: 8 (over z, x), sub: 4 (over y, core).
Axes of the slice: x: 2, y: 2, z: 4, core: 2. Of those that a mesh axis runs over, the one named last changes fastest.
Arguments:
- rhs: float32 [8192, 832], P(('dom', 'sub')), may hold values from -6 to 6
- elem_block: bfloat16 [8192, 64, 64], P(('dom', 'sub')), may hold values from -0.5 to 2.5
- block_inv: bfloat16 [8192, 64, 64], P(('dom', 'sub')), may hold values from -0.2 to 0.8
- flux_jac: float32 [13, 13], replicated, may hold values from -1.75 to 1.75
- face_src: int32 [8192, 6], P(('dom', 'sub')), may hold values from 0 to 2175
- send_face: int32 [160, 128], P(('dom', 'sub')), may hold values from 0 to 1535
- elem_route: int32 [8192], P(('dom', 'sub')), may hold values from 0 to 63
- agg_local: int32 [1024, 2], P(('dom', 'sub')), may hold values from 0 to 63
- coarse_block: float32 [2048, 4, 4], P(('dom', 'sub')), may hold values from -0.5 to 1.3
- coarse_inv: float32 [2048, 4, 4], P(('dom', 'sub')), may hold values from -1 to 4
Outputs:
- adjoint: float32 [8192, 832], P(('dom', 'sub'))
Inputs may be any that keep to these rules, and one draw needn't show every extreme that they name: `elem_route`: any owner may receive any slot from any device.
All inputs are finite; a program needn't handle non-finite values.
Results may differ from a plain program's by a relative error of at most 0.0081.
Values sent between devices are 32-bit elements; how exact they have to be, the bound alone decides.
A program may use at most 128 MiB of HBM per device.

v0:
```python
import functools
import math

import jax
import jax.numpy as jnp
import numpy as np
from jax import lax
from jax.experimental import pallas as pl
from jax.experimental.pallas import tpu as pltpu
from jax.sharding import PartitionSpec as P

COMPS = 13
NODES = 64
FACES = 6
FACE_NODES = 16
MODES = 4
ROUNDS = 5
MOST = 2
FLAT = COMPS * NODES
SIDE = COMPS * FACE_NODES
TRACE = FACES * SIDE

HIGHEST = lax.Precision.HIGHEST
PENALTY = 0.5
MESH = pl.DeviceIdType.MESH


def node_tables():
    points = np.array([-1.0, -1.0 / math.sqrt(5.0), 1.0 / math.sqrt(5.0), 1.0])
    weights = np.array([1.0, 5.0, 5.0, 1.0]) / 6.0
    grid_i, grid_j, grid_k = np.meshgrid(points, points, points, indexing="ij")
    weight_grid = weights[:, None, None] * weights[None, :, None] * weights[None, None, :] / 8.0
    basis = np.stack([np.ones(64), grid_i.reshape(-1), grid_j.reshape(-1), grid_k.reshape(-1)])
    restrict = basis * weight_grid.reshape(-1)[None, :]
    number = np.arange(64).reshape(4, 4, 4)
    sides = [number[0], number[3], number[:, 0], number[:, 3], number[:, :, 0], number[:, :, 3]]
    face_index = np.stack([side.reshape(-1) for side in sides])
    return basis, restrict, face_index


def const_tables():
    basis, restrict, face_index = node_tables()
    eye = np.eye(COMPS)
    row_comp = np.tile(np.repeat(eye, FACE_NODES, axis=0), (FACES, 1))
    row_comp = np.pad(row_comp, ((0, 0), (0, 3)))
    col_comp = np.pad(np.repeat(eye, NODES, axis=0), ((0, 0), (0, 3)))
    node = np.eye(NODES)[face_index]
    row_node = np.broadcast_to(node[:, None], (FACES, COMPS, FACE_NODES, NODES)).reshape(TRACE, NODES)
    col_node = np.tile(np.eye(NODES), (COMPS, 1))
    restrict_t = np.zeros((128, FLAT))
    restrict_t[: COMPS * MODES] = np.kron(eye, restrict)
    basis_t = np.zeros((FLAT, 128))
    basis_t[:, : COMPS * MODES] = np.kron(eye, basis.T)
    pick = np.zeros((128, MODES * 128))
    coef = np.zeros((16, MODES * 128))
    for k in range(MODES):
        for c in range(COMPS):
            for m in range(MODES):
                pick[c * MODES + k, k * 128 + c * MODES + m] = 1.0
                coef[m * MODES + k, k * 128 + c * MODES + m] = 1.0
    half = jnp.bfloat16
    return (
        jnp.asarray(row_comp, half),
        jnp.asarray(row_node, half),
        jnp.asarray(col_comp.T, half),
        jnp.asarray(col_node.T, half),
        jnp.asarray(col_comp, half),
        jnp.asarray(col_node, half),
        jnp.asarray(row_comp.T, half),
        jnp.asarray(row_node.T, half),
        jnp.asarray(restrict_t, jnp.float32),
        jnp.asarray(basis_t, jnp.float32),
        jnp.asarray(pick, jnp.float32),
        jnp.asarray(coef, jnp.float32),
    )


def dot(a, b):
    return jnp.dot(a, b, preferred_element_type=jnp.float32)


def dot_exact(a, b, dims=((1,), (0,))):
    return lax.dot_general(
        a, b, (dims, ((), ())), precision=HIGHEST, preferred_element_type=jnp.float32
    )


def kernel(
    count, subs,
    rhs, blocks, inverse, jac, face_src, send_face, route, agg_col, agg_row, cblock, cinv,
    row_comp, row_node, comp_col, node_col, col_comp, col_node, comp_row, node_row,
    restrict_t, basis_t, pick, coef,
    out,
    block_t, inverse_t, bcast, lift_t, trace_t, pick_local, pick_remote, pick_send,
    half_field, state, work, lifted, trace, beside, table, jump, sending, arriving,
    bucket, incoming, reply, answer,
    send_sem, recv_sem, give_sem, take_sem, back_sem, home_sem,
):
    elements = rhs.shape[1]
    tiles = elements // 128
    own = FACES * elements
    far = ROUNDS * 128
    me = lax.axis_index("dom") * subs + lax.axis_index("sub")

    def place(flat):
        return (flat // subs, flat % subs)

    def partner(k):
        bit = 1 << k
        return me + bit * (1 - 2 * ((me // bit) % 2))

    barrier = pltpu.get_barrier_semaphore()

    def greet(step, carry):
        pl.semaphore_signal(
            barrier, inc=1, device_id=place((me + step) % count), device_id_type=MESH
        )
        return carry

    lax.fori_loop(1, count, greet, 0)

    def swap(n, carry):
        for source, target in ((blocks, block_t), (inverse, inverse_t)):
            rows = source[n].astype(jnp.float32)
            for t in range(tiles):
                target[t, pl.ds(n, NODES, stride=NODES), :] = rows[:, t * 128 : (t + 1) * 128]
        return carry

    lax.fori_loop(0, NODES, swap, 0)

    def apply_blocks(source, emit):
        for t in range(tiles):
            def outer(pair, carry):
                base = pl.multiple_of(pair * 16, 16)

                def inner(step, total):
                    total = list(total)
                    for u in range(4):
                        k = step * 4 + u
                        low = source[t, pl.ds(k * NODES + base, 8), :]
                        high = source[t, pl.ds(k * NODES + base + 8, 8), :]
                        for c in range(COMPS):
                            value = bcast[t, pl.ds(c * NODES + k, 8, stride=0), :]
                            total[2 * c] = total[2 * c] + low * value
                            total[2 * c + 1] = total[2 * c + 1] + high * value
                    return tuple(total)

                zero = jnp.zeros((8, 128), jnp.float32)
                total = lax.fori_loop(0, NODES // 4, inner, (zero,) * (2 * COMPS))
                for c in range(COMPS):
                    for h in range(2):
                        rows = pl.ds(c * NODES + base + 8 * h, 8)
                        emit(rows, slice(t * 128, (t + 1) * 128), total[2 * c + h])
                return carry

            lax.fori_loop(0, NODES // 16, outer, 0)

    def spread(value):
        rounded = value.astype(jnp.bfloat16).astype(jnp.float32)
        for t in range(tiles):
            bcast[t] = rounded[:, t * 128 : (t + 1) * 128]

    def store(target):
        def emit(rows, lanes, value):
            target[rows, lanes] = value
        return emit

    spread(rhs[...])
    apply_blocks(inverse_t, store(state))

    jac_t = jac[...].astype(jnp.bfloat16)
    spread_jac = dot(jac_t, comp_col[...]).astype(jnp.bfloat16)

    def tables(f, carry):
        rows = pl.ds(pl.multiple_of(f * SIDE, SIDE), SIDE)
        value = dot(row_comp[rows, :], spread_jac) * dot(row_node[rows, :], node_col[...])
        trace_t[rows, :] = (PENALTY * value).astype(jnp.bfloat16)
        return carry

    lax.fori_loop(0, FACES, tables, 0)

    def lifts(i, carry):
        rows = pl.ds(pl.multiple_of(i * 208, 208), 208)
        value = dot(col_comp[rows, :], comp_row[...]) * dot(col_node[rows, :], node_row[...])
        lift_t[rows, :] = value.astype(jnp.bfloat16)
        return carry

    lax.fori_loop(0, FLAT // 208, lifts, 0)

    def column(row):
        element = (row * 43691) >> 18
        return jnp.where(row < own, (row - element * FACES) * elements + element, row)

    def one_hot(rows, wanted):
        index = lax.broadcasted_iota(jnp.int32, (rows, wanted.shape[1]), 0)
        return jnp.where(index == wanted, 1.0, 0.0).astype(jnp.bfloat16)

    for k in range(ROUNDS):
        pick_send[:, k * 128 : (k + 1) * 128] = one_hot(own, column(send_face[k : k + 1, :]))
    for f in range(FACES):
        wanted = column(face_src[f : f + 1, :])
        pick_local[f] = one_hot(own, wanted)
        pick_remote[f] = one_hot(far, wanted - own)
    route_row = (route[...] // MOST) * 8 + route[...] % MOST
    to_bucket = (
        lax.broadcasted_iota(jnp.int32, (count * 8, elements), 0) == route_row
    ).astype(jnp.float32)

    pl.semaphore_wait(barrier, count - 1)

    def operate(number):
        half_field[...] = state[...].astype(jnp.bfloat16)

        def traces(f, carry):
            rows = pl.ds(pl.multiple_of(f * SIDE, SIDE), SIDE)
            value = dot(trace_t[rows, :], half_field[...])
            trace[rows, :] = value
            table[:, pl.ds(pl.multiple_of(f * elements, 128), elements)] = value.astype(
                jnp.bfloat16
            )
            return carry

        lax.fori_loop(0, FACES, traces, 0)
        copies = []
        for k in range(ROUNDS):
            sending[k] = dot(table[:, :own], pick_send[:, k * 128 : (k + 1) * 128])
            copy = pltpu.make_async_remote_copy(
                src_ref=sending.at[k],
                dst_ref=arriving.at[number, k],
                send_sem=send_sem.at[number, k],
                recv_sem=recv_sem.at[number, k],
                device_id=place(partner(k)),
                device_id_type=MESH,
            )
            copy.start()
            copies.append(copy)
        spread(state[...])
        apply_blocks(block_t, store(work))

        def near(f, carry):
            rows = pl.ds(pl.multiple_of(f * SIDE, SIDE), SIDE)
            beside[rows, :] = trace[rows, :] - dot(table[:, :own], pick_local[f])
            return carry

        lax.fori_loop(0, FACES, near, 0)
        for k in range(ROUNDS):
            copies[k].wait()
            table[:, own + k * 128 : own + (k + 1) * 128] = arriving[number, k].astype(
                jnp.bfloat16
            )

        def beyond(f, carry):
            rows = pl.ds(pl.multiple_of(f * SIDE, SIDE), SIDE)
            value = beside[rows, :] - dot(table[:, own:], pick_remote[f])
            jump[rows, :] = value.astype(jnp.bfloat16)
            return carry

        lax.fori_loop(0, FACES, beyond, 0)

        def lift(i, carry):
            rows = pl.ds(pl.multiple_of(i * 208, 208), 208)
            lifted[rows, :] = rhs[rows, :] - work[rows, :] - dot(lift_t[rows, :], jump[...])
            return carry

        lax.fori_loop(0, FLAT // 208, lift, 0)

    def sweep(number, target):
        operate(number)
        spread(lifted[...])

        def emit(rows, lanes, value):
            target[rows, lanes] = state[rows, lanes] + value

        apply_blocks(inverse_t, emit)

    def exchange(source, target, sent, got):
        def copy_of(step):
            other = (me + step) % count
            return pltpu.make_async_remote_copy(
                src_ref=source.at[other],
                dst_ref=target.at[me],
                send_sem=sent.at[step],
                recv_sem=got.at[step],
                device_id=place(other),
                device_id_type=MESH,
            )

        def begin(step, carry):
            copy_of(step).start()
            return carry

        def finish(step, carry):
            copy_of(step).wait()
            return carry

        lax.fori_loop(1, count, begin, 0)
        target[me] = source[me]
        lax.fori_loop(1, count, finish, 0)

    sweep(0, state)
    operate(1)
    partial = dot_exact(restrict_t[...], lifted[...])
    bucket[...] = dot_exact(to_bucket, partial, ((1,), (1,))).reshape(count, 8, 128)
    exchange(bucket, incoming, give_sem, take_sem)
    owned = cblock.shape[0]
    gather_in = (
        lax.broadcasted_iota(jnp.int32, (owned, count * 8), 0) == agg_row[...]
    ).astype(jnp.float32)
    coarse_rhs = dot_exact(gather_in, incoming[...].reshape(count * 8, 128))
    inv_wide = dot_exact(cinv[...], coef[...])
    block_wide = dot_exact(cblock[...], coef[...])

    def modal(wide, value):
        product = wide * dot_exact(value, pick[...])
        return (
            product[:, :128] + product[:, 128:256] + product[:, 256:384] + product[:, 384:]
        )

    first = modal(inv_wide, coarse_rhs)
    solved = first + modal(inv_wide, coarse_rhs - modal(block_wide, first))
    gather_out = (
        lax.broadcasted_iota(jnp.int32, (count * 8, owned), 1) == agg_col[...]
    ).astype(jnp.float32)
    reply[...] = dot_exact(gather_out, solved).reshape(count, 8, 128)
    exchange(reply, answer, back_sem, home_sem)
    correction = dot_exact(answer[...].reshape(count * 8, 128), to_bucket, ((0,), (0,)))
    state[...] = state[...] + dot_exact(basis_t[...], correction)
    sweep(2, state)
    sweep(3, out)


def local(
    rhs,
    elem_block,
    block_inv,
    flux_jac,
    face_src,
    send_face,
    elem_route,
    agg_local,
    coarse_block,
    coarse_inv,
):
    elements = rhs.shape[0]
    count = lax.axis_size(("dom", "sub"))
    subs = lax.axis_size("sub")
    owned = coarse_block.shape[0]
    tiles = elements // 128
    own = FACES * elements
    far = ROUNDS * 128
    padded = jnp.pad(agg_local, ((0, 0), (0, 8 - MOST)), constant_values=-1)
    f32, half = jnp.float32, jnp.bfloat16
    dma = pltpu.SemaphoreType.DMA
    result = pl.pallas_call(
        functools.partial(kernel, count, subs),
        out_shape=jax.ShapeDtypeStruct((FLAT, elements), f32),
        in_specs=[pl.BlockSpec(memory_space=pltpu.VMEM)] * 23,
        out_specs=pl.BlockSpec(memory_space=pltpu.VMEM),
        scratch_shapes=[
            pltpu.VMEM((tiles, NODES * NODES, 128), f32),
            pltpu.VMEM((tiles, NODES * NODES, 128), f32),
            pltpu.VMEM((tiles, FLAT, 128), f32),
            pltpu.VMEM((FLAT, TRACE), half),
            pltpu.VMEM((TRACE, FLAT), half),
            pltpu.VMEM((FACES, own, elements), half),
            pltpu.VMEM((FACES, far, elements), half),
            pltpu.VMEM((own, far), half),
            pltpu.VMEM((FLAT, elements), half),
            pltpu.VMEM((FLAT, elements), f32),
            pltpu.VMEM((FLAT, elements), f32),
            pltpu.VMEM((FLAT, elements), f32),
            pltpu.VMEM((TRACE, elements), f32),
            pltpu.VMEM((TRACE, elements), f32),
            pltpu.VMEM((SIDE, own + far), half),
            pltpu.VMEM((TRACE, elements), half),
            pltpu.VMEM((ROUNDS, SIDE, 128), f32),
            pltpu.VMEM((4, ROUNDS, SIDE, 128), f32),
            pltpu.VMEM((count, 8, 128), f32),
            pltpu.VMEM((count, 8, 128), f32),
            pltpu.VMEM((count, 8, 128), f32),
            pltpu.VMEM((count, 8, 128), f32),
            dma((4, ROUNDS)),
            dma((4, ROUNDS)),
            dma((count,)),
            dma((count,)),
            dma((count,)),
            dma((count,)),
        ],
        compiler_params=pltpu.CompilerParams(
            collective_id=0, has_side_effects=True, vmem_limit_bytes=58 * 2**20
        ),
    )(
        rhs.T,
        elem_block.transpose(1, 2, 0),
        block_inv.transpose(1, 2, 0),
        jnp.pad(flux_jac.T, ((0, 3), (0, 3))),
        face_src.T,
        send_face,
        elem_route.reshape(1, elements),
        padded.reshape(count * 8, 1),
        padded.reshape(1, count * 8),
        coarse_block.reshape(owned, MODES * MODES),
        coarse_inv.reshape(owned, MODES * MODES),
        *const_tables(),
    )
    return result.T


def solution(mesh):
    return jax.shard_map(
        local,
        mesh=mesh,
        in_specs=(
            P(("dom", "sub"), None),
            P(("dom", "sub"), None, None),
            P(("dom", "sub"), None, None),
            P(),
            P(("dom", "sub"), None),
            P(("dom", "sub"), None),
            P(("dom", "sub")),
            P(("dom", "sub"), None),
            P(("dom", "sub"), None, None),
            P(("dom", "sub"), None, None),
        ),
        out_specs=P(("dom", "sub"), None),
        check_vma=False,
    )
```

profile of v0, /device:TPU:0, one launch (start us, length us, event | category | flops | bytes accessed | tf_op | source)
XLA Modules:
  0.0 120.3 jit_solution(7226125480026760248)
XLA Ops:
  0.0 0.8 copy.28
  0.8 0.6 pad.8.jac
  1.4 0.8 copy.34
  2.1 0.7 reshape.17.agg_row
  2.8 1.4 %copy.32.cblock = f32[64,16]{1,0:T(8,128)} copy(f32[64,16]{0,1:T(8,128)} %bitcast.14) | data formatting | bytes 8192 | tf_op jit(solution)/shard_map/reshape | solution.py:402
  4.2 1.4 %copy.33.cinv = f32[64,16]{1,0:T(8,128)} copy(f32[64,16]{0,1:T(8,128)} %bitcast.15) | data formatting | bytes 8192 | tf_op jit(solution)/shard_map/reshape | solution.py:403
  5.6 0.8 reshape.20.agg_col
  6.3 111.8 %shard_map.208 = f32[832,256]{1,0:T(8,128)} custom-call(f32[832,256]{1,0:T(8,128)} %bitcast.12, bf16[64,64,256]{2,1,0:T(8,128)(2,1)} %bitcast.10, bf16[64,64,256]{2,1,0:T(8,128)(2,1)} %bitcast.11, f32[16,16]{1,0:T(8,128)} %pad.8.jac, s32[6,256]{1,0:T(8,128)} %bitcast.16, s32[5,128]{1,0:T(8,128)} %send_face.1, s32[1,256]{1,0:T(1,128)} %bitcast.17, ...), custom_call_target="tpu_custom_call" | custom-call | tf_op jit(solution)/shard_map/pallas_call | solution.py:354
  118.1 2.1 %copy.36 = f32[256,832]{0,1:T(8,128)} copy(f32[256,832]{0,1:T(8,128)} %bitcast.9) | data formatting | bytes 1703936
  (1 shorter events, 0.0 us)
where the time goes:
time: 121 us; the launch traced here: 120 us
  Pallas kernels  112 us (93%)
  local copies, waits for them, and re-layouts  8.44 us (7%)
    pallas_call x1, Pallas kernels, local(): pl.pallas_call(functools.partial(kernel, count, subs), out_shape=jax.Shap...  112 us
    unnamed x3, local copies, waits for them, and re-layouts  3.65 us

commit v1 on v0

--- a/solution.py
+++ b/solution.py
@@ -17,6 +17,7 @@
 ROUNDS = 5
 MOST = 2
 FLAT = COMPS * NODES
+PITCH = NODES + 8
 SIDE = COMPS * FACE_NODES
 TRACE = FACES * SIDE
 
@@ -87,13 +88,13 @@
 
 def kernel(
     count, subs,
-    rhs, blocks, inverse, jac, face_src, send_face, route, agg_col, agg_row, cblock, cinv,
+    rhs, blocks, inverse, jac, face_src, send_face, route, agg_local, cblock, cinv,
     row_comp, row_node, comp_col, node_col, col_comp, col_node, comp_row, node_row,
     restrict_t, basis_t, pick, coef,
     out,
     block_t, inverse_t, bcast, lift_t, trace_t, pick_local, pick_remote, pick_send,
     half_field, state, work, lifted, trace, beside, table, jump, sending, arriving,
-    bucket, incoming, reply, answer,
+    bucket, incoming, reply, answer, jac_pad, flat_block, flat_inv,
     send_sem, recv_sem, give_sem, take_sem, back_sem, home_sem,
 ):
     elements = rhs.shape[1]
@@ -123,37 +124,38 @@
         for source, target in ((blocks, block_t), (inverse, inverse_t)):
             rows = source[n].astype(jnp.float32)
             for t in range(tiles):
-                target[t, pl.ds(n, NODES, stride=NODES), :] = rows[:, t * 128 : (t + 1) * 128]
+                target[t, pl.ds(n, NODES, stride=PITCH), :] = rows[:, t * 128 : (t + 1) * 128]
         return carry
 
     lax.fori_loop(0, NODES, swap, 0)
 
     def apply_blocks(source, emit):
         for t in range(tiles):
-            def outer(pair, carry):
-                base = pl.multiple_of(pair * 16, 16)
-
-                def inner(step, total):
-                    total = list(total)
-                    for u in range(4):
-                        k = step * 4 + u
-                        low = source[t, pl.ds(k * NODES + base, 8), :]
-                        high = source[t, pl.ds(k * NODES + base + 8, 8), :]
-                        for c in range(COMPS):
-                            value = bcast[t, pl.ds(c * NODES + k, 8, stride=0), :]
-                            total[2 * c] = total[2 * c] + low * value
-                            total[2 * c + 1] = total[2 * c + 1] + high * value
-                    return tuple(total)
-
-                zero = jnp.zeros((8, 128), jnp.float32)
-                total = lax.fori_loop(0, NODES // 4, inner, (zero,) * (2 * COMPS))
-                for c in range(COMPS):
-                    for h in range(2):
-                        rows = pl.ds(c * NODES + base + 8 * h, 8)
-                        emit(rows, slice(t * 128, (t + 1) * 128), total[2 * c + h])
+            def outer(quad, carry):
+                base = pl.multiple_of(quad * 32, 32)
+                for comps in (range(0, 7), range(7, COMPS)):
+                    def inner(step, total):
+                        total = list(total)
+                        for u in range(4):
+                            k = step * 4 + u
+                            parts = [
+                                source[t, pl.ds(k * PITCH + base + 8 * h, 8), :] for h in range(4)
+                            ]
+                            for i, c in enumerate(comps):
+                                value = bcast[t, pl.ds(c * NODES + k, 8, stride=0), :]
+                                for h in range(4):
+                                    total[4 * i + h] = total[4 * i + h] + parts[h] * value
+                        return tuple(total)
+
+                    zero = jnp.zeros((8, 128), jnp.float32)
+                    total = lax.fori_loop(0, NODES // 4, inner, (zero,) * (4 * len(comps)))
+                    for i, c in enumerate(comps):
+                        for h in range(4):
+                            rows = pl.ds(c * NODES + base + 8 * h, 8)
+                            emit(rows, slice(t * 128, (t + 1) * 128), total[4 * i + h])
                 return carry
 
-            lax.fori_loop(0, NODES // 16, outer, 0)
+            lax.fori_loop(0, NODES // 32, outer, 0)
 
     def spread(value):
         rounded = value.astype(jnp.bfloat16).astype(jnp.float32)
@@ -168,8 +170,19 @@
     spread(rhs[...])
     apply_blocks(inverse_t, store(state))
 
-    jac_t = jac[...].astype(jnp.bfloat16)
-    spread_jac = dot(jac_t, comp_col[...]).astype(jnp.bfloat16)
+    jac_pad[...] = jnp.zeros_like(jac_pad)
+    jac_pad[:COMPS, :COMPS] = jac[...]
+    spread_jac = lax.dot_general(
+        jac_pad[...].astype(jnp.bfloat16),
+        comp_col[...],
+        (((0,), (0,)), ((), ())),
+        preferred_element_type=jnp.float32,
+    )[:16].astype(jnp.bfloat16)
+    for m in range(MODES):
+        flat_block[m * MODES : (m + 1) * MODES, :] = cblock[m]
+        flat_inv[m * MODES : (m + 1) * MODES, :] = cinv[m]
+    inv_wide = dot_exact(flat_inv[...], coef[...], ((0,), (0,)))
+    block_wide = dot_exact(flat_block[...], coef[...], ((0,), (0,)))
 
     def tables(f, carry):
         rows = pl.ds(pl.multiple_of(f * SIDE, SIDE), SIDE)
@@ -211,19 +224,21 @@
     def operate(number):
         half_field[...] = state[...].astype(jnp.bfloat16)
 
-        def traces(f, carry):
-            rows = pl.ds(pl.multiple_of(f * SIDE, SIDE), SIDE)
+        def traces(third, carry):
+            rows = pl.ds(pl.multiple_of(third * 2 * SIDE, 2 * SIDE), 2 * SIDE)
             value = dot(trace_t[rows, :], half_field[...])
             trace[rows, :] = value
-            table[:, pl.ds(pl.multiple_of(f * elements, 128), elements)] = value.astype(
-                jnp.bfloat16
-            )
-            return carry
-
-        lax.fori_loop(0, FACES, traces, 0)
+            column_pair = pl.ds(pl.multiple_of(third * 2 * elements, 128), elements)
+            table[:, column_pair] = value[:SIDE].astype(jnp.bfloat16)
+            column_pair = pl.ds(pl.multiple_of((third * 2 + 1) * elements, 128), elements)
+            table[:, column_pair] = value[SIDE:].astype(jnp.bfloat16)
+            return carry
+
+        lax.fori_loop(0, FACES // 2, traces, 0)
+        outgoing = dot(table[:, :own], pick_send[...])
         copies = []
         for k in range(ROUNDS):
-            sending[k] = dot(table[:, :own], pick_send[:, k * 128 : (k + 1) * 128])
+            sending[k] = outgoing[:, k * 128 : (k + 1) * 128]
             copy = pltpu.make_async_remote_copy(
                 src_ref=sending.at[k],
                 dst_ref=arriving.at[number, k],
@@ -258,11 +273,11 @@
         lax.fori_loop(0, FACES, beyond, 0)
 
         def lift(i, carry):
-            rows = pl.ds(pl.multiple_of(i * 208, 208), 208)
+            rows = pl.ds(pl.multiple_of(i * 416, 416), 416)
             lifted[rows, :] = rhs[rows, :] - work[rows, :] - dot(lift_t[rows, :], jump[...])
             return carry
 
-        lax.fori_loop(0, FLAT // 208, lift, 0)
+        lax.fori_loop(0, FLAT // 416, lift, 0)
 
     def sweep(number, target):
         operate(number)
@@ -302,13 +317,14 @@
     partial = dot_exact(restrict_t[...], lifted[...])
     bucket[...] = dot_exact(to_bucket, partial, ((1,), (1,))).reshape(count, 8, 128)
     exchange(bucket, incoming, give_sem, take_sem)
-    owned = cblock.shape[0]
-    gather_in = (
-        lax.broadcasted_iota(jnp.int32, (owned, count * 8), 0) == agg_row[...]
-    ).astype(jnp.float32)
-    coarse_rhs = dot_exact(gather_in, incoming[...].reshape(count * 8, 128))
-    inv_wide = dot_exact(cinv[...], coef[...])
-    block_wide = dot_exact(cblock[...], coef[...])
+    owned = cblock.shape[2]
+    members = [
+        (
+            lax.broadcasted_iota(jnp.int32, (owned, count), 0) == agg_local[s : s + 1, :]
+        ).astype(jnp.float32)
+        for s in range(MOST)
+    ]
+    coarse_rhs = sum(dot_exact(members[s], incoming[:, s, :]) for s in range(MOST))
 
     def modal(wide, value):
         product = wide * dot_exact(value, pick[...])
@@ -318,15 +334,18 @@
 
     first = modal(inv_wide, coarse_rhs)
     solved = first + modal(inv_wide, coarse_rhs - modal(block_wide, first))
-    gather_out = (
-        lax.broadcasted_iota(jnp.int32, (count * 8, owned), 1) == agg_col[...]
-    ).astype(jnp.float32)
-    reply[...] = dot_exact(gather_out, solved).reshape(count, 8, 128)
+    reply[...] = jnp.zeros_like(reply)
+    for s in range(MOST):
+        reply[:, s, :] = dot_exact(members[s], solved, ((0,), (0,)))
     exchange(reply, answer, back_sem, home_sem)
     correction = dot_exact(answer[...].reshape(count * 8, 128), to_bucket, ((0,), (0,)))
     state[...] = state[...] + dot_exact(basis_t[...], correction)
-    sweep(2, state)
-    sweep(3, out)
+    def last_sweeps(number, carry):
+        sweep(number, state)
+        return carry
+
+    lax.fori_loop(2, 4, last_sweeps, 0)
+    out[...] = state[...]
 
 
 def local(
@@ -348,17 +367,16 @@
     tiles = elements // 128
     own = FACES * elements
     far = ROUNDS * 128
-    padded = jnp.pad(agg_local, ((0, 0), (0, 8 - MOST)), constant_values=-1)
     f32, half = jnp.float32, jnp.bfloat16
     dma = pltpu.SemaphoreType.DMA
     result = pl.pallas_call(
         functools.partial(kernel, count, subs),
         out_shape=jax.ShapeDtypeStruct((FLAT, elements), f32),
-        in_specs=[pl.BlockSpec(memory_space=pltpu.VMEM)] * 23,
+        in_specs=[pl.BlockSpec(memory_space=pltpu.VMEM)] * 22,
         out_specs=pl.BlockSpec(memory_space=pltpu.VMEM),
         scratch_shapes=[
-            pltpu.VMEM((tiles, NODES * NODES, 128), f32),
-            pltpu.VMEM((tiles, NODES * NODES, 128), f32),
+            pltpu.VMEM((tiles, NODES * PITCH, 128), f32),
+            pltpu.VMEM((tiles, NODES * PITCH, 128), f32),
             pltpu.VMEM((tiles, FLAT, 128), f32),
             pltpu.VMEM((FLAT, TRACE), half),
             pltpu.VMEM((TRACE, FLAT), half),
@@ -379,6 +397,9 @@
             pltpu.VMEM((count, 8, 128), f32),
             pltpu.VMEM((count, 8, 128), f32),
             pltpu.VMEM((count, 8, 128), f32),
+            pltpu.VMEM((16, 128), f32),
+            pltpu.VMEM((MODES * MODES, owned), f32),
+            pltpu.VMEM((MODES * MODES, owned), f32),
             dma((4, ROUNDS)),
             dma((4, ROUNDS)),
             dma((count,)),
@@ -393,14 +414,13 @@
         rhs.T,
         elem_block.transpose(1, 2, 0),
         block_inv.transpose(1, 2, 0),
-        jnp.pad(flux_jac.T, ((0, 3), (0, 3))),
+        flux_jac,
         face_src.T,
         send_face,
         elem_route.reshape(1, elements),
-        padded.reshape(count * 8, 1),
-        padded.reshape(1, count * 8),
-        coarse_block.reshape(owned, MODES * MODES),
-        coarse_inv.reshape(owned, MODES * MODES),
+        agg_local.T,
+        coarse_block.transpose(1, 2, 0),
+        coarse_inv.transpose(1, 2, 0),
         *const_tables(),
     )
     return result.T

time: 121 us -> 100 us (0.83)
  Pallas kernels: 112 us -> 98.1 us
  local copies, waits for them, and re-layouts: 8.44 us -> 2.11 us
    pallas_call x1, Pallas kernels: 112 us -> 98.1 us  [local(): pl.pallas_call(functools.partial(kernel, count, subs), out_shape=jax.Shap...]
    reshape x4 -> x0, local copies, waits for them, and re-layouts: 4.19 us -> none  [the longest x1 1.38 us: local(): coarse_inv.reshape(owned, MODES * MODES)]
    unnamed x3 -> x1, local copies, waits for them, and re-layouts: 3.65 us -> 2.11 us
where the time goes in v1:
time: 100 us
  Pallas kernels  98.1 us (98%)
  local copies, waits for them, and re-layouts  2.11 us (2%)
    pallas_call x1, Pallas kernels, local(): pl.pallas_call(functools.partial(kernel, count, subs), out_shape=jax.Shap...  98.1 us
    unnamed x1, local copies, waits for them, and re-layouts  2.11 us

profile of v1, /device:TPU:0, one launch (start us, length us, event | category | flops | bytes accessed | tf_op | source)
XLA Modules:
  0.0 100.2 jit_solution(16056633252105569528)
XLA Ops:
  0.0 98.1 %shard_map.208 = f32[832,256]{1,0:T(8,128)} custom-call(f32[832,256]{1,0:T(8,128)} %bitcast.12, bf16[64,64,256]{2,1,0:T(8,128)(2,1)} %bitcast.10, bf16[64,64,256]{2,1,0:T(8,128)(2,1)} %bitcast.11, f32[13,13]{1,0:T(8,128)} %jac.1, s32[6,256]{1,0:T(8,128)} %bitcast.13, s32[5,128]{1,0:T(8,128)} %send_face.1, s32[1,256]{1,0:T(1,128)} %bitcast.16, ...), custom_call_target="tpu_custom_call" | custom-call | tf_op jit(solution)/shard_map/pallas_call | solution.py:372
  98.1 2.1 %copy.24 = f32[256,832]{0,1:T(8,128)} copy(f32[256,832]{0,1:T(8,128)} %bitcast.9) | data formatting | bytes 1703936
